TPU v7x, 32 devices: a whole 2x2x4 slice. The times are simulated.
32 devices in a mesh: groups: 2 (over x), ctx: 4 (over y, core), head: 4 (over z).
Axes of the slice: x: 2, y: 2, z: 4, core: 2. Of those that a mesh axis runs over, the one named last changes fastest.
Arguments:
- hidden: bfloat16 [2, 2048, 4096], P(None, ('groups', 'ctx'), 'head'), parts along dimension 1, may hold values from -40 to 40
- strand_bases: int32 [2048], P(('groups', 'ctx')), parts along dimension 0, may hold values from 0 to 3
- variant_sites: int32 [256], P('groups'), parts along dimension 0, may hold values from 0 to 1023, as said below
- base_shift: int32 [256], P('groups'), parts along dimension 0, may hold values from 1 to 3
- base_embed: bfloat16 [4, 4096], replicated, may hold values from -6 to 6
- query_weight: bfloat16 [4096, 2048], P(None, 'head')
- key_weight: bfloat16 [4096, 2048], P(None, 'head')
- value_weight: bfloat16 [4096, 2048], P(None, 'head'), may hold values from -0.09375 to 0.09375
- out_weight: bfloat16 [2048, 4096], P('head'), may hold values from -4 to 4
Outputs:
- mixed: bfloat16 [2048, 4096], P(('groups', 'ctx'), 'head'), parts along dimension 0
There are 2 independent parts, one for each index of `groups`. A program takes and returns all parts, laid end to end along the dimension named above; an argument that names none is the same for every part. Nothing has to cross between parts.
Inputs may be any that keep to these rules, and one draw needn't show every extreme that they name: `variant_sites`: distinct positions; each aligned block of 256 positions holds at most 64 of them, and some block holds exactly that many.
All inputs are finite; a program needn't handle non-finite values.
Results may differ from a plain program's by a relative error of at most 0.019.
Values may be sent and summed in bfloat16 or wider, within the bound.
A program may use at most 128 MiB of HBM per device.

v0:
```python
import functools
import math

import jax
import jax.numpy as jnp
from jax import lax
from jax.experimental import pallas as pl
from jax.experimental.pallas import tpu as pltpu
from jax.sharding import PartitionSpec as P

HEAD_DIM = 128
VAR_DEV = 32
ROPE_BASE = 10000.0
NEG_FILL = -1e30
FAR = 1 << 29
PIECES = 2
MESH = pl.DeviceIdType.MESH
VMEM_LIMIT = 60 * 1024 * 1024


def greet(axis, size):
    me = lax.axis_index(axis)
    barrier = pltpu.get_barrier_semaphore()

    @pl.when(me > 0)
    def _():
        pl.semaphore_signal(barrier, inc=1, device_id={axis: me - 1}, device_id_type=MESH)

    @pl.when(me < size - 1)
    def _():
        pl.semaphore_signal(barrier, inc=1, device_id={axis: me + 1}, device_id_type=MESH)

    pl.semaphore_wait(barrier, jnp.minimum(me, 1) + jnp.minimum(size - 1 - me, 1))


def project_kernel(
    size,
    hidden,
    wq,
    wk,
    wv,
    sel,
    sel_t,
    has_row,
    codes,
    table,
    cos,
    sin,
    q_out,
    kv_out,
    xbuf,
    wbuf,
    stk,
    acc,
    own_sem,
    w_sem,
    s_sem,
    r_sem,
):
    z = lax.axis_index("head")
    rows, feats = hidden.shape[1], hidden.shape[2]
    slots = sel.shape[0]
    hw = wq.shape[1]
    heads = hw // HEAD_DIM
    piece = rows // PIECES

    greet("head", size)

    def hop(side, strand, shard, part, source):
        span = pl.ds(part * piece, piece)
        return pltpu.make_async_remote_copy(
            src_ref=source.at[strand, span] if source is hidden else xbuf.at[strand, shard, span],
            dst_ref=xbuf.at[strand, shard, span],
            send_sem=s_sem.at[side, strand, shard, part],
            recv_sem=r_sem.at[strand, shard, part],
            device_id={"head": z - 1 if side == 0 else z + 1},
            device_id_type=MESH,
        )

    def send_own(side, strand):
        for part in range(PIECES):
            hop(side, strand, z, part, hidden).start()

    for strand in range(1):

        @pl.when(z > 0)
        def _():
            send_own(0, strand)

        @pl.when(z < size - 1)
        def _():
            send_own(1, strand)

    @pl.when((z > 0) & (z == size - 1))
    def _():
        send_own(0, 1)

    @pl.when((z < size - 1) & (z == 0))
    def _():
        send_own(1, 1)

    own = [
        pltpu.make_async_copy(hidden.at[strand], xbuf.at[strand, z], own_sem.at[strand])
        for strand in range(2)
    ]
    loads = [
        pltpu.make_async_copy(weight, wbuf.at[index], w_sem.at[index])
        for index, weight in enumerate((wq, wk, wv))
    ]
    for copy in own + loads:
        copy.start()
    for copy in own + loads:
        copy.wait()

    shorter = jnp.minimum(z, size - 1 - z)
    long_side = jnp.where(z < size - 1 - z, 1, -1)

    def shard_of(step):
        paired = jnp.where(step % 2 == 1, (step + 1) // 2, -((step + 1) // 2))
        return z + jnp.where(step <= 2 * shorter, paired, long_side * (step - shorter))

    for strand in range(2):
        acc[...] = jnp.zeros_like(acc)

        def step_body(step, carry):
            shard = shard_of(step)
            for part in range(PIECES):

                @pl.when(shard > z)
                def _():
                    hop(0, strand, shard, part, xbuf).wait_recv()

                    @pl.when(z > 0)
                    def _():
                        hop(0, strand, shard, part, xbuf).start()

                @pl.when(shard < z)
                def _():
                    hop(1, strand, shard, part, xbuf).wait_recv()

                    @pl.when(z < size - 1)
                    def _():
                        hop(1, strand, shard, part, xbuf).start()

            if strand == 0:

                @pl.when((shard == size - 1) & (z < size - 1) & (z > 0))
                def _():
                    send_own(0, 1)

                @pl.when((shard == 0) & (z > 0) & (z < size - 1))
                def _():
                    send_own(1, 1)

            block = xbuf[strand, shard]
            stk[pl.ds(0, rows), :] = block
            first = pl.multiple_of(shard * feats, feats)
            diff = jnp.zeros((slots, feats), jnp.float32)
            for code in range(4):
                diff = diff + codes[strand][:, code : code + 1] * table[
                    pl.ds(code, 1), pl.ds(first, feats)
                ]
            picked = jnp.dot(sel[...], block, preferred_element_type=jnp.float32)
            stk[pl.ds(rows, slots), :] = (picked + diff).astype(jnp.bfloat16)
            for index in range(3):
                acc[:, pl.ds(index * hw, hw)] += jnp.dot(
                    stk[...],
                    wbuf[index, pl.ds(first, feats), :],
                    preferred_element_type=jnp.float32,
                )
            return carry

        lax.fori_loop(0, size, step_body, 0)

        cos_part = cos[strand]
        sin_part = sin[strand]
        for head in range(heads):
            cols = pl.ds(head * HEAD_DIM, HEAD_DIM)
            for index in range(2):
                raw = acc[:, pl.ds(index * hw + head * HEAD_DIM, HEAD_DIM)]
                turned = raw * cos_part + pltpu.roll(raw, HEAD_DIM // 2, 1) * sin_part
                turned = turned.astype(jnp.bfloat16)
                if index == 0:
                    base = turned[:rows]
                    placed = jnp.dot(
                        sel_t[...], turned[rows:], preferred_element_type=jnp.float32
                    )
                    q_out[strand, 0, :, cols] = base
                    q_out[strand, 1, :, cols] = jnp.where(
                        has_row[...] > 0.5, placed, base.astype(jnp.float32)
                    ).astype(jnp.bfloat16)
                else:
                    kv_out[strand, :, cols] = turned
        kv_out[strand, :, pl.ds(hw, hw)] = acc[:, pl.ds(2 * hw, hw)].astype(jnp.bfloat16)

    def drain(step, carry):
        shard = shard_of(step)
        for strand in range(2):
            for part in range(PIECES):

                @pl.when((shard >= z) & (z > 0))
                def _():
                    hop(0, strand, shard, part, xbuf).wait_send()

                @pl.when((shard <= z) & (z < size - 1))
                def _():
                    hop(1, strand, shard, part, xbuf).wait_send()

        return carry

    lax.fori_loop(0, size, drain, 0)


def attend_kernel(size, q_in, kv_in, kt_mut, out, kvbuf, m_buf, l_buf, a_buf, s_sem, r_sem):
    me = lax.axis_index("ctx")
    rows, hw = q_in.shape[2], q_in.shape[3]
    heads = hw // HEAD_DIM
    wide = kv_in.shape[1]
    window = rows * size
    log_scale = math.log2(math.e) / math.sqrt(HEAD_DIM)

    greet("ctx", size)

    def hop(strand, shard, own):
        return pltpu.make_async_remote_copy(
            src_ref=kv_in.at[strand] if own else kvbuf.at[strand, shard],
            dst_ref=kvbuf.at[strand, shard],
            send_sem=s_sem.at[strand, shard],
            recv_sem=r_sem.at[strand, shard],
            device_id={"ctx": me + 1 if strand == 0 else me - 1},
            device_id_type=MESH,
        )

    passes_on = (me < size - 1, me > 0)
    for strand in range(2):

        @pl.when(passes_on[strand])
        def _():
            hop(strand, me, True).start()

    row_iota = lax.broadcasted_iota(jnp.int32, (rows, 1), 0)
    col_iota = lax.broadcasted_iota(jnp.int32, (1, rows), 1)

    def clock(strand, block, iota):
        place = block * rows + iota
        return place if strand == 0 else window - 1 - place

    def update(strand, shard, block, first):
        q_time = clock(strand, me, row_iota)
        k_times = (clock(strand, shard, col_iota), kt_mut[strand, shard])
        spans = (rows, wide)

        def one_head(head, carry):
            k_cols = pl.ds(pl.multiple_of(head * HEAD_DIM, HEAD_DIM), HEAD_DIM)
            v_cols = pl.ds(pl.multiple_of(hw + head * HEAD_DIM, HEAD_DIM), HEAD_DIM)
            for kind in range(2):
                span = pl.ds(0, spans[kind])
                raw = lax.dot_general(
                    q_in[strand, kind, :, k_cols],
                    block[span, k_cols],
                    (((1,), (1,)), ((), ())),
                    preferred_element_type=jnp.float32,
                )
                raw = jnp.where(k_times[kind] <= q_time, raw, NEG_FILL)
                top = jnp.max(raw, axis=1, keepdims=True)
                if not first:
                    old = m_buf[strand, head, kind]
                    top = jnp.maximum(old, top)
                    fade = jnp.exp2((old - top) * log_scale)
                weights = jnp.exp2((raw - top) * log_scale)
                total = jnp.sum(weights, axis=1, keepdims=True)
                vec = jnp.dot(
                    weights.astype(jnp.bfloat16),
                    block[span, v_cols],
                    preferred_element_type=jnp.float32,
                )
                if not first:
                    total = total + fade * l_buf[strand, head, kind]
                    vec = vec + fade * a_buf[strand, head, kind]
                m_buf[strand, head, kind] = top
                l_buf[strand, head, kind] = total
                a_buf[strand, head, kind] = vec
            return carry

        lax.fori_loop(0, heads, one_head, 0)

    for strand in range(2):
        update(strand, me, kv_in.at[strand], True)

    def arrive(step, carry):
        shards = (me - step, me + step)
        live = (me - step >= 0, me + step < size)
        for strand in range(2):

            @pl.when(live[strand])
            def _():
                hop(strand, shards[strand], False).wait_recv()

                @pl.when(passes_on[strand])
                def _():
                    hop(strand, shards[strand], False).start()

                update(strand, shards[strand], kvbuf.at[strand, shards[strand]], False)

        return carry

    lax.fori_loop(1, size, arrive, 0)

    for head in range(heads):
        part = [
            a_buf[strand, head, kind] / l_buf[strand, head, kind]
            for strand in range(2)
            for kind in range(2)
        ]
        out[:, pl.ds(head * HEAD_DIM, HEAD_DIM)] = (
            0.5 * ((part[0] - part[1]) + (part[2] - part[3]))
        ).astype(jnp.bfloat16)

    def drain(step, carry):
        shards = (me - step, me + step)
        live = (me - step >= 0, me + step < size)
        for strand in range(2):

            @pl.when(live[strand] & passes_on[strand])
            def _():
                hop(strand, shards[strand], False).wait_send()

        return carry

    lax.fori_loop(0, size, drain, 0)


def vmem():
    return pl.BlockSpec(memory_space=pltpu.VMEM)


def anywhere():
    return pl.BlockSpec(memory_space=pl.ANY)


def shards(
    hidden,
    strand_bases,
    variant_sites,
    base_shift,
    base_embed,
    query_weight,
    key_weight,
    value_weight,
    out_weight,
):
    rows, feats = hidden.shape[1], hidden.shape[2]
    n_head = lax.axis_size("head")
    n_ctx = lax.axis_size("ctx")
    window = rows * n_ctx
    me = lax.axis_index("ctx")
    start = me * rows
    slots = 2 * VAR_DEV
    wide = rows + slots
    hw = query_weight.shape[1]
    heads = hw // HEAD_DIM
    width = query_weight.shape[0]

    count = variant_sites.shape[0]
    order = jnp.arange(count, dtype=jnp.int32)
    row_iota = jnp.arange(rows, dtype=jnp.int32)
    v_block = variant_sites // rows
    before = (v_block[:, None] == v_block[None, :]) & (order[None, :] < order[:, None])
    rank = jnp.sum(before.astype(jnp.int32), axis=1)
    mine = v_block == me
    slot_iota = jnp.arange(slots, dtype=jnp.int32)
    slot_match = (rank[:, None] == slot_iota[None, :]) & mine[:, None]
    row_match = ((variant_sites - start)[:, None] == row_iota[None, :]) & mine[:, None]
    old_base = jnp.sum(jnp.where(row_match, strand_bases[None, :], 0), axis=1)
    new_base = jnp.mod(old_base + base_shift, 4)
    slot_old = jnp.sum(jnp.where(slot_match, old_base[:, None], 0), axis=0)
    slot_new = jnp.sum(jnp.where(slot_match, new_base[:, None], 0), axis=0)
    slot_live = jnp.any(slot_match, axis=0)
    has_row = jnp.any(row_match, axis=0).astype(jnp.float32)[:, None]

    all_slot = v_block * slots + rank
    all_match = all_slot[:, None] == jnp.arange(n_ctx * slots, dtype=jnp.int32)[None, :]
    all_pos = jnp.sum(jnp.where(all_match, variant_sites[:, None], 0), axis=0)
    all_live = jnp.any(all_match, axis=0)
    slot_pos = jnp.sum(jnp.where(slot_match, variant_sites[:, None], 0), axis=0)
    place = jnp.arange(window, dtype=jnp.int32)
    has_key = jnp.any(variant_sites[:, None] == place[None, :], axis=0)
    kt_mut = jnp.stack(
        [
            jnp.concatenate(
                [
                    jnp.where(has_key, FAR, flip(place)).reshape(n_ctx, rows),
                    jnp.where(all_live, flip(all_pos), FAR).reshape(n_ctx, slots),
                ],
                axis=1,
            )
            for flip in (lambda p: p, lambda p: window - 1 - p)
        ]
    )[:, :, None, :]

    sel = (
        (jnp.where(slot_live, slot_pos - start, -1)[:, None] == row_iota[None, :])
    ).astype(jnp.bfloat16)
    sel_t = (
        (row_iota[:, None] == jnp.where(slot_live, slot_pos - start, -1)[None, :])
    ).astype(jnp.bfloat16)
    code_iota = jnp.arange(4, dtype=jnp.int32)

    def signed(new, old):
        hot = (new[:, None] == code_iota[None, :]).astype(jnp.float32) - (
            old[:, None] == code_iota[None, :]
        ).astype(jnp.float32)
        return jnp.where(slot_live[:, None], hot, 0.0)

    codes = jnp.stack([signed(slot_new, slot_old), signed(3 - slot_new, 3 - slot_old)])
    table = base_embed.astype(jnp.float32)

    plus_pos = jnp.concatenate([start + row_iota, slot_pos])
    pos = jnp.stack([plus_pos, window - 1 - plus_pos]).astype(jnp.float32)
    half = HEAD_DIM // 2
    freq = jnp.power(ROPE_BASE, -jnp.arange(half, dtype=jnp.float32) * 2.0 / HEAD_DIM)
    angle = pos[:, :, None] * freq[None, None, :]
    cos_half, sin_half = jnp.cos(angle), jnp.sin(angle)
    cos = jnp.concatenate([cos_half, cos_half], axis=-1)
    sin = jnp.concatenate([-sin_half, sin_half], axis=-1)

    queries, cache = pl.pallas_call(
        functools.partial(project_kernel, n_head),
        out_shape=(
            jax.ShapeDtypeStruct((2, 2, rows, hw), jnp.bfloat16),
            jax.ShapeDtypeStruct((2, wide, 2 * hw), jnp.bfloat16),
        ),
        in_specs=[anywhere()] * 4 + [vmem()] * 7,
        out_specs=(vmem(), vmem()),
        scratch_shapes=[
            pltpu.VMEM((2, n_head, rows, feats), jnp.bfloat16),
            pltpu.VMEM((3, width, hw), jnp.bfloat16),
            pltpu.VMEM((wide, feats), jnp.bfloat16),
            pltpu.VMEM((wide, 3 * hw), jnp.float32),
            pltpu.SemaphoreType.DMA((2,)),
            pltpu.SemaphoreType.DMA((3,)),
            pltpu.SemaphoreType.DMA((2, 2, n_head, PIECES)),
            pltpu.SemaphoreType.DMA((2, n_head, PIECES)),
        ],
        compiler_params=pltpu.CompilerParams(
            collective_id=0, has_side_effects=True, vmem_limit_bytes=VMEM_LIMIT
        ),
        name="project",
    )(
        hidden,
        query_weight,
        key_weight,
        value_weight,
        sel,
        sel_t,
        has_row,
        codes,
        table,
        cos,
        sin,
    )

    combined = pl.pallas_call(
        functools.partial(attend_kernel, n_ctx),
        out_shape=jax.ShapeDtypeStruct((rows, hw), jnp.bfloat16),
        in_specs=[vmem()] * 3,
        out_specs=vmem(),
        scratch_shapes=[
            pltpu.VMEM((2, n_ctx, wide, 2 * hw), jnp.bfloat16),
            pltpu.VMEM((2, heads, 2, rows, 1), jnp.float32),
            pltpu.VMEM((2, heads, 2, rows, 1), jnp.float32),
            pltpu.VMEM((2, heads, 2, rows, HEAD_DIM), jnp.float32),
            pltpu.SemaphoreType.DMA((2, n_ctx)),
            pltpu.SemaphoreType.DMA((2, n_ctx)),
        ],
        compiler_params=pltpu.CompilerParams(
            collective_id=1, has_side_effects=True, vmem_limit_bytes=VMEM_LIMIT
        ),
        name="attend",
    )(queries, cache, kt_mut)

    summed = lax.psum_scatter(
        lax.dot_general(
            out_weight, combined, (((0,), (1,)), ((), ())), preferred_element_type=jnp.float32
        ).astype(jnp.bfloat16),
        "head",
        scatter_dimension=0,
        tiled=True,
    ).astype(jnp.float32)
    return summed.T.astype(jnp.bfloat16)


def solution(mesh):
    return jax.shard_map(
        shards,
        mesh=mesh,
        in_specs=(
            P(None, ("groups", "ctx"), "head"),
            P(("groups", "ctx")),
            P("groups"),
            P("groups"),
            P(),
            P(None, "head"),
            P(None, "head"),
            P(None, "head"),
            P("head", None),
        ),
        out_specs=P(("groups", "ctx"), "head"),
        check_vma=False,
    )
```

profile of v0, /device:TPU:0, one launch (start us, length us, event | category | flops | bytes accessed | tf_op | source)
XLA Modules:
  0.0 186.1 jit_solution(18107384813995759428)
XLA Ops:
  6.5 0.7 broadcast_compare_fusion
  7.2 0.7 broadcast_subtract_fusion.2
  7.9 0.2 convert_reduce_fusion
  8.1 0.1 fusion.10
  8.2 0.9 select_reduce_fusion.1
  9.0 0.7 and_select_fusion
  9.7 0.8 select_reduce_fusion.3
  10.5 0.7 fusion.3.sel_t
  11.2 0.7 fusion.8.sel
  11.9 0.1 fusion.5
  12.0 0.8 select_reduce_fusion
  12.8 0.1 fusion.2
  12.9 0.8 fusion.1
  13.8 0.7 copy.14.codes
  14.5 0.8 copy.13.has_row
  15.3 1.4 convert_element_type.92.table
  16.7 0.1 reduce_or.45
  16.9 0.6 broadcast_in_dim.128.kt_mut
  17.5 1.2 fusion.6
  18.7 1.1 pad_maximum_fusion
  19.8 77.8 %project.1 = (bf16[2,2,256,512]{3,2,1,0:T(8,128)(2,1)}, bf16[2,320,1024]{2,1,0:T(8,128)(2,1)}) custom-call(bf16[2,256,1024]{2,1,0:T(8,128)(2,1)} %hidden.1, bf16[4096,512]{1,0:T(8,128)(2,1)} %wq.1, bf16[4096,512]{1,0:T(8,128)(2,1)} %wk.1, bf16[4096,512]{1,0:T(8,128)(2,1)} %wv.1, bf16[64,256]{1,0:T(8,128)(2,1)} %fusion.8.sel, bf16[256,64]{1,0:T(8,128)(2,1)} %fusion.3.sel_t, ...), custom_call_target="tpu_custom_call" | custom-call | tf_op jit(solution)/shard_map/project/pallas_call | solution.py:427
  97.6 32.2 %attend.1 = bf16[256,512]{1,0:T(8,128)(2,1)} custom-call(bf16[2,2,256,512]{3,2,1,0:T(8,128)(2,1)} %get-tuple-element.7.q_in, bf16[2,320,1024]{2,1,0:T(8,128)(2,1)} %get-tuple-element.8.kv_in, s32[2,4,1,320]{3,2,1,0:T(1,128)} %broadcast_in_dim.128.kt_mut), custom_call_target="tpu_custom_call" | custom-call | tf_op jit(solution)/shard_map/attend/pallas_call | solution.py:463
  129.8 4.9 %fusion = bf16[4096,256]{0,1:T(8,128)(2,1)} fusion(bf16[256,512]{1,0:T(8,128)(2,1)} %attend.1, bf16[512,4096]{1,0:T(8,128)(2,1)} %param.17), kind=kOutput, calls=%fused_computation.1 | convolution fusion | flops 1074790400 | bytes 6553600 | tf_op jit(solution)/shard_map/dot_general | solution.py:483
  134.7 44.5 %reduce-scatter.2.cloned.1.call-done = bf16[1024,256]{0,1:T(8,128)(2,1)} async-done(((bf16[4096,256]{0,1:T(8,128)(2,1)}), bf16[1024,256]{0,1:T(8,128)(2,1)}) %reduce-scatter.2.cloned.1.call-update) | async-done | bytes 524304 | tf_op jit(solution)/shard_map/reduce_scatter | solution.py:482
  (20 shorter events, 0.2 us)
Async XLA Ops:
  6.5 172.7 %reduce-scatter.2.cloned.1.call-start = ((), (), s32[]{:S(2)}) async-start(), calls=%async_computation.1 | async-start | bytes 2621440 | tf_op jit(solution)/shard_map/reduce_scatter | solution.py:482
Sparse Core Ops, SparseCore 0:
  134.8 44.3 reduce-scatter.1
where the time goes:
time: 186 us
  Pallas kernels  110 us (59%)
  waiting for transfers between devices  44.6 us (24%)
  between operations  13.5 us (7%)
  other arithmetic  10.9 us (6%)
  matrix products  4.89 us (3%)
  local copies, waits for them, and re-layouts  2.3 us (1%)
    pallas_call x1, Pallas kernels, shards(): pl.pallas_call(functools.partial(project_kernel, n_head), out_shape=(jax....  77.8 us
    reduce_scatter x1, waiting for transfers between devices, shards(): lax.psum_scatter(lax.dot_general(out_weight, combined, (((0,), (1,)), (()...  44.5 us
    pallas_call x1, Pallas kernels, shards(): pl.pallas_call(functools.partial(attend_kernel, n_ctx), out_shape=jax.Sha...  32.2 us
    dot_general x1, matrix products, shards(): lax.dot_general(out_weight, combined, (((0,), (1,)), ((), ())), preferred...  4.89 us
  transfers between devices with their start and end apart: 1, of which 1 were waited for; matrix products, arithmetic and copies ran while one was open for 0% of the time, Pallas kernels for 0%

commit v1 on v0

v1 whole, which is shorter than its diff:
```python
import functools
import math

import jax
import jax.numpy as jnp
import numpy as np
from jax import lax
from jax.experimental import pallas as pl
from jax.experimental.pallas import tpu as pltpu
from jax.sharding import PartitionSpec as P

HEAD_DIM = 128
VAR_DEV = 32
ROPE_BASE = 10000.0
NEG_FILL = -1e30
FAR = 1e9
PIECES = 2
MESH = pl.DeviceIdType.MESH
VMEM_LIMIT = 62 * 1024 * 1024


def iota(shape, axis):
    return lax.broadcasted_iota(jnp.int32, shape, axis).astype(jnp.float32)


def center_out(count):
    half = count // 2
    if count % 2:
        return [(half,)] + [(half - k, half + k) for k in range(1, half + 1)]
    return [(half - 1 - k, half + k) for k in range(half)]


def fused_kernel(
    n_groups,
    n_ctx,
    n_head,
    hidden,
    bases_in,
    sites_in,
    shifts_in,
    embed_in,
    freq_in,
    wq,
    wk,
    wv,
    wo_in,
    out,
    xbuf,
    wbuf,
    wo_own,
    wo_far,
    bases,
    sites,
    shifts,
    embed,
    freq,
    stk,
    acc,
    diff,
    sel,
    sel_t,
    has_row,
    kt,
    cos,
    sin,
    qbuf,
    kvbuf,
    m_buf,
    l_buf,
    a_buf,
    part,
    comb,
    mix,
    small_sem,
    own_sem,
    w_sem,
    xs_sem,
    xr_sem,
    ws_sem,
    wr_sem,
    ps_sem,
    pr_sem,
    ks_sem,
    kr_sem,
    cs_sem,
    cr_sem,
):
    g = lax.axis_index("groups")
    me = lax.axis_index("ctx")
    z = lax.axis_index("head")
    rows, feats = hidden.shape[1], hidden.shape[2]
    hw = wq.shape[1]
    heads = hw // HEAD_DIM
    slots = 2 * VAR_DEV
    window = rows * n_ctx
    piece = rows // PIECES
    plane = n_groups * n_ctx
    place = g * n_ctx + me
    log_scale = math.log2(math.e) / math.sqrt(HEAD_DIM)

    barrier = pltpu.get_barrier_semaphore()

    def greet_line(step, carry):
        other = lax.rem(z + step, n_head)
        pl.semaphore_signal(barrier, inc=1, device_id={"head": other}, device_id_type=MESH)
        return carry

    def greet_plane(step, carry):
        other = lax.rem(place + step, plane)
        pl.semaphore_signal(
            barrier,
            inc=1,
            device_id={"groups": other // n_ctx, "ctx": lax.rem(other, n_ctx)},
            device_id_type=MESH,
        )
        return carry

    lax.fori_loop(1, n_head, greet_line, 0)
    lax.fori_loop(1, plane, greet_plane, 0)
    pl.semaphore_wait(barrier, n_head - 1 + plane - 1)

    part_rows, part_cols = hw // n_ctx, feats // n_groups

    def part_span(owner_group, owner_ctx):
        return (
            pl.ds(pl.multiple_of(owner_ctx * part_rows, part_rows), part_rows),
            pl.ds(pl.multiple_of(owner_group * part_cols, part_cols), part_cols),
        )

    def fetch(step):
        other = lax.rem(z + step, n_head)
        span = part_span(g, me)
        first = pl.multiple_of(other * feats + g * part_cols, part_cols)
        return pltpu.make_async_remote_copy(
            src_ref=wo_in.at[span[0], pl.ds(first, part_cols)],
            dst_ref=wo_far.at[n_head - step - 1, span[0], span[1]],
            send_sem=ws_sem.at[n_head - step - 1],
            recv_sem=wr_sem.at[n_head - step - 1],
            device_id={"head": other},
            device_id_type=MESH,
        )

    def share(step):
        other = lax.rem(place + step, plane)
        span = part_span(g, me)
        return pltpu.make_async_remote_copy(
            src_ref=wo_far.at[:, span[0], span[1]],
            dst_ref=wo_far.at[:, span[0], span[1]],
            send_sem=ps_sem.at[step - 1],
            recv_sem=pr_sem.at[step - 1],
            device_id={"groups": other // n_ctx, "ctx": lax.rem(other, n_ctx)},
            device_id_type=MESH,
        )

    def shared_from(step):
        other = lax.rem(place + plane - step, plane)
        span = part_span(other // n_ctx, lax.rem(other, n_ctx))
        return pltpu.make_async_remote_copy(
            src_ref=wo_far.at[:, span[0], span[1]],
            dst_ref=wo_far.at[:, span[0], span[1]],
            send_sem=ps_sem.at[step - 1],
            recv_sem=pr_sem.at[step - 1],
            device_id={"groups": other // n_ctx, "ctx": lax.rem(other, n_ctx)},
            device_id_type=MESH,
        )

    for step in range(1, n_head):
        fetch(step).start()

    def hop(side, strand, shard, part_id, source):
        span = pl.ds(part_id * piece, piece)
        return pltpu.make_async_remote_copy(
            src_ref=source.at[strand, span] if source is hidden else xbuf.at[strand, shard, span],
            dst_ref=xbuf.at[strand, shard, span],
            send_sem=xs_sem.at[side, strand, shard, part_id],
            recv_sem=xr_sem.at[strand, shard, part_id],
            device_id={"head": z - 1 if side == 0 else z + 1},
            device_id_type=MESH,
        )

    def send_own(side, strand):
        for part_id in range(PIECES):
            hop(side, strand, z, part_id, hidden).start()

    @pl.when(z > 0)
    def _():
        send_own(0, 0)

    @pl.when(z < n_head - 1)
    def _():
        send_own(1, 0)

    @pl.when((z > 0) & (z == n_head - 1))
    def _():
        send_own(0, 1)

    @pl.when((z < n_head - 1) & (z == 0))
    def _():
        send_own(1, 1)

    smalls = [
        pltpu.make_async_copy(source, target, small_sem.at[index])
        for index, (source, target) in enumerate(
            (
                (bases_in, bases),
                (sites_in, sites),
                (shifts_in, shifts),
                (embed_in, embed),
                (freq_in, freq),
            )
        )
    ]
    own = [
        pltpu.make_async_copy(hidden.at[strand], xbuf.at[strand, z], own_sem.at[strand])
        for strand in range(2)
    ]
    loads = [
        pltpu.make_async_copy(weight, wbuf.at[index], w_sem.at[index])
        for index, weight in enumerate((wq, wk, wv))
    ]
    load_out = pltpu.make_async_copy(
        wo_in.at[:, pl.ds(pl.multiple_of(z * feats, feats), feats)], wo_own, w_sem.at[3]
    )
    for copy in smalls + own + loads + [load_out]:
        copy.start()
    for copy in smalls:
        copy.wait()

    start = (me * rows).astype(jnp.float32)
    here = me.astype(jnp.float32)
    v_row = sites[...].astype(jnp.float32)
    count = v_row.shape[1]
    v_col = jnp.sum(
        jnp.where(iota((count, count), 0) == iota((count, count), 1), v_row, 0.0),
        axis=1,
        keepdims=True,
    )

    def block_of(positions):
        total = jnp.zeros_like(positions)
        for edge in range(1, n_ctx):
            total = total + jnp.where(positions >= float(edge * rows), 1.0, 0.0)
        return total

    b_row, b_col = block_of(v_row), block_of(v_col)
    same = b_col == b_row
    rank_col = jnp.sum(jnp.where(same & (v_row < v_col), 1.0, 0.0), axis=1, keepdims=True)
    rank_row = jnp.sum(jnp.where(same & (v_col < v_row), 1.0, 0.0), axis=0, keepdims=True)
    slot_col, slot_row = iota((slots, 1), 0), iota((1, slots), 1)
    row_col, row_row = iota((rows, 1), 0), iota((1, rows), 1)

    match = (slot_col == rank_row) & (b_row == here)
    live_col = jnp.max(jnp.where(match, 1.0, 0.0), axis=1, keepdims=True)
    pos_col = jnp.sum(jnp.where(match, v_row, 0.0), axis=1, keepdims=True)
    shift_col = jnp.sum(
        jnp.where(match, shifts[...].astype(jnp.float32), 0.0), axis=1, keepdims=True
    )
    match_t = (rank_col == slot_row) & (b_col == here)
    live_row = jnp.max(jnp.where(match_t, 1.0, 0.0), axis=0, keepdims=True)
    pos_row = jnp.sum(jnp.where(match_t, v_col, 0.0), axis=0, keepdims=True)
    spot_col = jnp.where(live_col > 0.5, pos_col - start, -1.0)
    spot_row = jnp.where(live_row > 0.5, pos_row - start, -1.0)
    picks = spot_col == row_row
    sel[...] = jnp.where(picks, 1.0, 0.0).astype(jnp.bfloat16)
    places = jnp.where(row_col == spot_row, 1.0, 0.0)
    sel_t[...] = places.astype(jnp.bfloat16)
    has_row[...] = jnp.max(places, axis=1, keepdims=True)
    old = jnp.sum(
        jnp.where(picks, bases[...].astype(jnp.float32), 0.0), axis=1, keepdims=True
    )
    new = old + shift_col
    new = jnp.where(new > 3.5, new - 4.0, new)
    for strand in range(2):
        total = jnp.zeros((slots, embed.shape[1]), jnp.float32)
        for code in range(4):
            want = float(code if strand == 0 else 3 - code)
            coef = jnp.where(new == want, 1.0, 0.0) - jnp.where(old == want, 1.0, 0.0)
            coef = jnp.where(live_col > 0.5, coef, 0.0)
            total = total + coef * embed[pl.ds(code, 1), :].astype(jnp.float32)
        diff[strand] = total

    def clock(strand, where):
        return where if strand == 0 else float(window - 1) - where

    for shard in range(n_ctx):
        hit = (rank_col == slot_row) & (b_col == float(shard))
        live = jnp.max(jnp.where(hit, 1.0, 0.0), axis=0, keepdims=True)
        where_slot = jnp.sum(jnp.where(hit, v_col, 0.0), axis=0, keepdims=True)
        where_key = row_row + float(shard * rows)
        changed = jnp.max(jnp.where(v_col == where_key, 1.0, 0.0), axis=0, keepdims=True)
        for strand in range(2):
            kt[strand, shard, :, pl.ds(0, rows)] = jnp.where(
                changed > 0.5, FAR, clock(strand, where_key)
            )
            kt[strand, shard, :, pl.ds(rows, slots)] = jnp.where(
                live > 0.5, clock(strand, where_slot), FAR
            )

    lane = lax.broadcasted_iota(jnp.int32, (1, HEAD_DIM), 1)
    turn = jnp.where(lane < HEAD_DIM // 2, -1.0, 1.0)
    for strand in range(2):
        for span, where in (
            (pl.ds(0, rows), row_col + start),
            (pl.ds(rows, slots), pos_col),
        ):
            angle = clock(strand, where) * freq[...]
            cos[strand, span, :] = jnp.cos(angle)
            sin[strand, span, :] = jnp.sin(angle) * turn

    for copy in own + loads:
        copy.wait()

    shorter = jnp.minimum(z, n_head - 1 - z)
    long_side = jnp.where(z < n_head - 1 - z, 1, -1)

    def shard_of(step):
        paired = jnp.where(step % 2 == 1, (step + 1) // 2, -((step + 1) // 2))
        return z + jnp.where(step <= 2 * shorter, paired, long_side * (step - shorter))

    def project(strand):
        acc[...] = jnp.zeros_like(acc)

        def step_body(step, carry):
            shard = shard_of(step)
            for part_id in range(PIECES):

                @pl.when(shard > z)
                def _():
                    hop(0, strand, shard, part_id, xbuf).wait_recv()

                    @pl.when(z > 0)
                    def _():
                        hop(0, strand, shard, part_id, xbuf).start()

                @pl.when(shard < z)
                def _():
                    hop(1, strand, shard, part_id, xbuf).wait_recv()

                    @pl.when(z < n_head - 1)
                    def _():
                        hop(1, strand, shard, part_id, xbuf).start()

            if strand == 0:

                @pl.when((shard == n_head - 1) & (z < n_head - 1) & (z > 0))
                def _():
                    send_own(0, 1)

                @pl.when((shard == 0) & (z > 0) & (z < n_head - 1))
                def _():
                    send_own(1, 1)

                @pl.when(step == 1)
                def _():
                    for far in range(1, n_head):
                        fetch(far).wait_recv()

                    def spread(other, inner):
                        share(other).start()
                        return inner

                    lax.fori_loop(1, plane, spread, 0)

            block = xbuf[strand, shard]
            stk[pl.ds(0, rows), :] = block
            first = pl.multiple_of(shard * feats, feats)
            picked = jnp.dot(sel[...], block, preferred_element_type=jnp.float32)
            stk[pl.ds(rows, slots), :] = (
                picked + diff[strand, :, pl.ds(first, feats)]
            ).astype(jnp.bfloat16)
            for index in range(3):
                acc[:, pl.ds(index * hw, hw)] += jnp.dot(
                    stk[...],
                    wbuf[index, pl.ds(first, feats), :],
                    preferred_element_type=jnp.float32,
                )
            return carry

        lax.fori_loop(0, n_head, step_body, 0)

    passes_on = (me < n_ctx - 1, me > 0)

    def pass_kv(strand, shard, head):
        return pltpu.make_async_remote_copy(
            src_ref=kvbuf.at[strand, shard, head],
            dst_ref=kvbuf.at[strand, shard, head],
            send_sem=ks_sem.at[strand, shard, head],
            recv_sem=kr_sem.at[strand, shard, head],
            device_id={"ctx": me + 1 if strand == 0 else me - 1},
            device_id_type=MESH,
        )

    def rotated(strand, index, head):
        raw = acc[:, pl.ds(index * hw + head * HEAD_DIM, HEAD_DIM)]
        return (
            raw * cos[strand] + pltpu.roll(raw, HEAD_DIM // 2, 1) * sin[strand]
        ).astype(jnp.bfloat16)

    def finish(strand):
        def send_head(head):
            @pl.when(passes_on[strand])
            def _():
                pass_kv(strand, me, head).start()

        for head in range(heads):
            kvbuf[strand, me, head, :, pl.ds(0, HEAD_DIM)] = rotated(strand, 1, head)
            kvbuf[strand, me, head, :, pl.ds(HEAD_DIM, HEAD_DIM)] = acc[
                :, pl.ds(2 * hw + head * HEAD_DIM, HEAD_DIM)
            ].astype(jnp.bfloat16)
            if head:
                send_head(head - 1)
        for head in range(heads):
            turned = rotated(strand, 0, head)
            base = turned[:rows]
            placed = jnp.dot(sel_t[...], turned[rows:], preferred_element_type=jnp.float32)
            qbuf[0, head] = base
            qbuf[1, head] = jnp.where(
                has_row[...] > 0.5, placed, base.astype(jnp.float32)
            ).astype(jnp.bfloat16)
            if head == 0:
                send_head(heads - 1)

    def comb_hop(side, shard, head):
        cols = pl.ds(pl.multiple_of(head * HEAD_DIM, HEAD_DIM), HEAD_DIM)
        return pltpu.make_async_remote_copy(
            src_ref=comb.at[shard, :, cols],
            dst_ref=comb.at[shard, :, cols],
            send_sem=cs_sem.at[side, shard, head],
            recv_sem=cr_sem.at[shard, head],
            device_id={"head": z - 1 if side == 0 else z + 1},
            device_id_type=MESH,
        )

    def send_comb(head):
        @pl.when(z > 0)
        def _():
            comb_hop(0, z, head).start()

        @pl.when(z < n_head - 1)
        def _():
            comb_hop(1, z, head).start()

    def attend(strand):
        q_time = clock(strand, row_col + start)

        def update(shard, head, first):
            k_times = (clock(strand, row_row + (shard * rows).astype(jnp.float32)), kt[strand, shard])
            spans = (rows, rows + slots)
            for kind in range(2):
                span = pl.ds(0, spans[kind])
                raw = lax.dot_general(
                    qbuf[kind, head],
                    kvbuf[strand, shard, head, span, pl.ds(0, HEAD_DIM)],
                    (((1,), (1,)), ((), ())),
                    preferred_element_type=jnp.float32,
                )
                if first or kind == 1:
                    raw = jnp.where(k_times[kind] <= q_time, raw, NEG_FILL)
                top = jnp.max(raw, axis=1, keepdims=True)
                if not first:
                    before = m_buf[kind]
                    top = jnp.maximum(before, top)
                    fade = jnp.exp2((before - top) * log_scale)
                weights = jnp.exp2((raw - top) * log_scale)
                total = jnp.sum(weights, axis=1, keepdims=True)
                vec = jnp.dot(
                    weights.astype(jnp.bfloat16),
                    kvbuf[strand, shard, head, span, pl.ds(HEAD_DIM, HEAD_DIM)],
                    preferred_element_type=jnp.float32,
                )
                if not first:
                    total = total + fade * l_buf[kind]
                    vec = vec + fade * a_buf[kind]
                m_buf[kind] = top
                l_buf[kind] = total
                a_buf[kind] = vec

        def one_head(head, carry):
            update(me, head, True)

            def arrive(step, inner):
                shard = me - step if strand == 0 else me + step

                @pl.when(shard >= 0 if strand == 0 else shard < n_ctx)
                def _():
                    pass_kv(strand, shard, head).wait_recv()

                    @pl.when(passes_on[strand])
                    def _():
                        pass_kv(strand, shard, head).start()

                    update(shard, head, False)

                return inner

            lax.fori_loop(1, n_ctx, arrive, 0)
            gap = a_buf[0] / l_buf[0] - a_buf[1] / l_buf[1]
            if strand == 0:
                part[head] = gap
            else:
                cols = pl.ds(pl.multiple_of(head * HEAD_DIM, HEAD_DIM), HEAD_DIM)
                comb[z, :, cols] = (0.5 * (part[head] + gap)).astype(jnp.bfloat16)
                send_comb(head)
            return carry

        lax.fori_loop(0, heads, one_head, 0)

    for strand in range(2):
        project(strand)
        finish(strand)
        attend(strand)

    load_out.wait()
    mix[...] = jnp.dot(comb[z], wo_own[...], preferred_element_type=jnp.float32)

    def collect(step, carry):
        shared_from(step).wait_recv()
        return carry

    lax.fori_loop(1, plane, collect, 0)
    for pair in center_out(n_head):
        for head in range(heads):
            for shard in pair:

                @pl.when(z < shard)
                def _():
                    comb_hop(0, shard, head).wait_recv()

                    @pl.when(z > 0)
                    def _():
                        comb_hop(0, shard, head).start()

                @pl.when(z > shard)
                def _():
                    comb_hop(1, shard, head).wait_recv()

                    @pl.when(z < n_head - 1)
                    def _():
                        comb_hop(1, shard, head).start()

        for shard in pair:

            @pl.when(z != shard)
            def _():
                mix[...] += jnp.dot(
                    comb[shard],
                    wo_far[lax.rem(shard - z - 1 + n_head, n_head)],
                    preferred_element_type=jnp.float32,
                )

    out[...] = mix[...].astype(jnp.bfloat16)

    for step in range(1, n_head):
        fetch(step).wait_send()

    def drain_share(step, carry):
        share(step).wait_send()
        return carry

    lax.fori_loop(1, plane, drain_share, 0)

    def drain_line(shard, carry):
        @pl.when((shard >= z) & (z > 0))
        def _():
            for strand in range(2):
                for part_id in range(PIECES):
                    hop(0, strand, shard, part_id, xbuf).wait_send()
            for head in range(heads):
                comb_hop(0, shard, head).wait_send()

        @pl.when((shard <= z) & (z < n_head - 1))
        def _():
            for strand in range(2):
                for part_id in range(PIECES):
                    hop(1, strand, shard, part_id, xbuf).wait_send()
            for head in range(heads):
                comb_hop(1, shard, head).wait_send()

        return carry

    lax.fori_loop(0, n_head, drain_line, 0)

    def drain_ctx(shard, carry):
        for strand in range(2):

            @pl.when(passes_on[strand] & (shard <= me if strand == 0 else shard >= me))
            def _():
                for head in range(heads):
                    pass_kv(strand, shard, head).wait_send()

        return carry

    lax.fori_loop(0, n_ctx, drain_ctx, 0)


def anywhere():
    return pl.BlockSpec(memory_space=pl.ANY)


def shards(
    hidden,
    strand_bases,
    variant_sites,
    base_shift,
    base_embed,
    query_weight,
    key_weight,
    value_weight,
    out_weight,
):
    rows, feats = hidden.shape[1], hidden.shape[2]
    n_groups = lax.axis_size("groups")
    n_ctx = lax.axis_size("ctx")
    n_head = lax.axis_size("head")
    slots = 2 * VAR_DEV
    wide = rows + slots
    hw = query_weight.shape[1]
    heads = hw // HEAD_DIM
    width = query_weight.shape[0]
    count = variant_sites.shape[0]
    plane = n_groups * n_ctx

    half = HEAD_DIM // 2
    freq = np.power(np.float32(ROPE_BASE), -np.arange(half, dtype=np.float32) * 2.0 / HEAD_DIM)
    freq = np.concatenate([freq, freq]).astype(np.float32)[None, :]

    f32, bf16, i32 = jnp.float32, jnp.bfloat16, jnp.int32
    dma = pltpu.SemaphoreType.DMA
    return pl.pallas_call(
        functools.partial(fused_kernel, n_groups, n_ctx, n_head),
        out_shape=jax.ShapeDtypeStruct((rows, feats), bf16),
        in_specs=[anywhere()] * 10,
        out_specs=pl.BlockSpec(memory_space=pltpu.VMEM),
        scratch_shapes=[
            pltpu.VMEM((2, n_head, rows, feats), bf16),
            pltpu.VMEM((3, width, hw), bf16),
            pltpu.VMEM((hw, feats), bf16),
            pltpu.VMEM((max(n_head - 1, 1), hw, feats), bf16),
            pltpu.VMEM((1, rows), i32),
            pltpu.VMEM((1, count), i32),
            pltpu.VMEM((1, count), i32),
            pltpu.VMEM((4, width), bf16),
            pltpu.VMEM((1, HEAD_DIM), f32),
            pltpu.VMEM((wide, feats), bf16),
            pltpu.VMEM((wide, 3 * hw), f32),
            pltpu.VMEM((2, slots, width), f32),
            pltpu.VMEM((slots, rows), bf16),
            pltpu.VMEM((rows, slots), bf16),
            pltpu.VMEM((rows, 1), f32),
            pltpu.VMEM((2, n_ctx, 1, wide), f32),
            pltpu.VMEM((2, wide, HEAD_DIM), f32),
            pltpu.VMEM((2, wide, HEAD_DIM), f32),
            pltpu.VMEM((2, heads, rows, HEAD_DIM), bf16),
            pltpu.VMEM((2, n_ctx, heads, wide, 2 * HEAD_DIM), bf16),
            pltpu.VMEM((2, rows, 1), f32),
            pltpu.VMEM((2, rows, 1), f32),
            pltpu.VMEM((2, rows, HEAD_DIM), f32),
            pltpu.VMEM((heads, rows, HEAD_DIM), f32),
            pltpu.VMEM((n_head, rows, hw), bf16),
            pltpu.VMEM((rows, feats), f32),
            dma((5,)),
            dma((2,)),
            dma((4,)),
            dma((2, 2, n_head, PIECES)),
            dma((2, n_head, PIECES)),
            dma((max(n_head - 1, 1),)),
            dma((max(n_head - 1, 1),)),
            dma((plane,)),
            dma((plane,)),
            dma((2, n_ctx, heads)),
            dma((2, n_ctx, heads)),
            dma((2, n_head, heads)),
            dma((n_head, heads)),
        ],
        compiler_params=pltpu.CompilerParams(
            collective_id=0, has_side_effects=True, vmem_limit_bytes=VMEM_LIMIT
        ),
        name="fused",
    )(
        hidden,
        strand_bases[None, :],
        variant_sites[None, :],
        base_shift[None, :],
        base_embed,
        jnp.asarray(freq),
        query_weight,
        key_weight,
        value_weight,
        out_weight,
    )


def solution(mesh):
    return jax.shard_map(
        shards,
        mesh=mesh,
        in_specs=(
            P(None, ("groups", "ctx"), "head"),
            P(("groups", "ctx")),
            P("groups"),
            P("groups"),
            P(),
            P(None, "head"),
            P(None, "head"),
            P(None, "head"),
            P("head", None),
        ),
        out_specs=P(("groups", "ctx"), "head"),
        check_vma=False,
    )
```

time: 186 us -> 161 us (0.87)
  Pallas kernels: 110 us -> 159 us
  waiting for transfers between devices: 44.6 us -> 0 us
  between operations: 13.5 us -> 0.01 us
  other arithmetic: 10.9 us -> 0 us
  matrix products: 4.89 us -> 0 us
    pallas_call x2 -> x1, Pallas kernels: 110 us -> 159 us  [shards(): pl.pallas_call(functools.partial(fused_kernel, n_groups, n_ctx, n_head),...]
    reduce_scatter x1 -> x0, waiting for transfers between devices: 44.5 us -> none  [shards(): lax.psum_scatter(lax.dot_general(out_weight, combined, (((0,), (1,)), (()...]
    dot_general x1 -> x0, matrix products: 4.89 us -> none  [shards(): lax.dot_general(out_weight, combined, (((0,), (1,)), ((), ())), preferred...]
    convert_element_type x5 -> x0, other arithmetic: 2.74 us -> none  [the longest x1 1.38 us: shards(): table = base_embed.astype(jnp.float32)]
    reduce_sum x4 -> x0, other arithmetic: 2.61 us -> none  [the longest x1 0.87 us: shards(): old_base = jnp.sum(jnp.where(row_match, strand_bases[None, :], 0), axis=1)]
    unnamed x0 -> x1, local copies, waits for them, and re-layouts: none -> 1.87 us
  transfers between devices with their start and end apart: 1 -> 0, of which waited for: 1 -> 0; matrix products, arithmetic and copies ran while one was open for 0% -> 0% of each run, Pallas kernels for 0% -> 0%
where the time goes in v1:
time: 161 us
  Pallas kernels  159 us (99%)
  local copies, waits for them, and re-layouts  1.87 us (1%)
    pallas_call x1, Pallas kernels, shards(): pl.pallas_call(functools.partial(fused_kernel, n_groups, n_ctx, n_head),...  159 us

profile of v1, /device:TPU:0, one launch (start us, length us, event | category | flops | bytes accessed | tf_op | source)
XLA Modules:
  0.0 160.6 jit_solution(9277442668442212007)
XLA Ops:
  0.0 158.7 %fused.1 = bf16[256,1024]{1,0:T(8,128)(2,1)} custom-call(bf16[2,256,1024]{2,1,0:T(8,128)(2,1)} %hidden.1, s32[1,256]{1,0:T(1,128)} %bitcast.3, s32[1,128]{1,0:T(1,128)} %bitcast.4, s32[1,128]{1,0:T(1,128)} %bitcast.5, bf16[4,4096]{1,0:T(4,128)(2,1)} %embed_in.1, f32[1,128]{1,0:T(1,128)} %constant.2.clone.freq_in, bf16[4096,512]{1,0:T(8,128)(2,1)} %wq.1, ...), custom_call_target="tpu_custom_call" | custom-call | tf_op jit(solution)/shard_map/fused/pallas_call | solution.py:629
  158.7 1.9 %copy.12 = bf16[256,1024]{1,0:T(8,128)(2,1)} copy(bf16[256,1024]{1,0:T(8,128)(2,1)} %fused.1) | data formatting | bytes 1048576

commit v2 on v1

--- a/solution.py
+++ b/solution.py
@@ -26,7 +26,7 @@
 def center_out(count):
     half = count // 2
     if count % 2:
-        return [(half,)] + [(half - k, half + k) for k in range(1, half + 1)]
+        return [(half, half)] + [(half - k, half + k) for k in range(1, half + 1)]
     return [(half - 1 - k, half + k) for k in range(half)]
 
 
@@ -413,8 +413,8 @@
             turned = rotated(strand, 0, head)
             base = turned[:rows]
             placed = jnp.dot(sel_t[...], turned[rows:], preferred_element_type=jnp.float32)
-            qbuf[0, head] = base
-            qbuf[1, head] = jnp.where(
+            qbuf[strand, 0, head] = base
+            qbuf[strand, 1, head] = jnp.where(
                 has_row[...] > 0.5, placed, base.astype(jnp.float32)
             ).astype(jnp.bfloat16)
             if head == 0:
@@ -449,7 +449,7 @@
             for kind in range(2):
                 span = pl.ds(0, spans[kind])
                 raw = lax.dot_general(
-                    qbuf[kind, head],
+                    qbuf[strand, kind, head],
                     kvbuf[strand, shard, head, span, pl.ds(0, HEAD_DIM)],
                     (((1,), (1,)), ((), ())),
                     preferred_element_type=jnp.float32,
@@ -505,10 +505,22 @@
 
         lax.fori_loop(0, heads, one_head, 0)
 
-    for strand in range(2):
-        project(strand)
-        finish(strand)
-        attend(strand)
+    at_end = (z == 0) | (z == n_head - 1)
+    project(0)
+    finish(0)
+
+    @pl.when(at_end)
+    def _():
+        attend(0)
+
+    project(1)
+    finish(1)
+
+    @pl.when(jnp.logical_not(at_end))
+    def _():
+        attend(0)
+
+    attend(1)
 
     load_out.wait()
     mix[...] = jnp.dot(comb[z], wo_own[...], preferred_element_type=jnp.float32)
@@ -518,27 +530,33 @@
         return carry
 
     lax.fori_loop(1, plane, collect, 0)
-    for pair in center_out(n_head):
-        for head in range(heads):
-            for shard in pair:
-
-                @pl.when(z < shard)
-                def _():
-                    comb_hop(0, shard, head).wait_recv()
-
-                    @pl.when(z > 0)
-                    def _():
-                        comb_hop(0, shard, head).start()
-
-                @pl.when(z > shard)
-                def _():
-                    comb_hop(1, shard, head).wait_recv()
-
-                    @pl.when(z < n_head - 1)
-                    def _():
-                        comb_hop(1, shard, head).start()
-
-        for shard in pair:
+
+    def pass_comb(shard, head):
+        @pl.when(z < shard)
+        def _():
+            comb_hop(0, shard, head).wait_recv()
+
+            @pl.when(z > 0)
+            def _():
+                comb_hop(0, shard, head).start()
+
+        @pl.when(z > shard)
+        def _():
+            comb_hop(1, shard, head).wait_recv()
+
+            @pl.when(z < n_head - 1)
+            def _():
+                comb_hop(1, shard, head).start()
+
+    for low, high in center_out(n_head):
+        near = jnp.where(2 * z < n_head, low, high)
+        for head in range(heads + 1):
+            if head < heads:
+                pass_comb(near, head)
+            if head and low != high:
+                pass_comb(low + high - near, head - 1)
+
+        for shard in (low, high)[: 1 + (low != high)]:
 
             @pl.when(z != shard)
             def _():
@@ -650,7 +668,7 @@
             pltpu.VMEM((2, n_ctx, 1, wide), f32),
             pltpu.VMEM((2, wide, HEAD_DIM), f32),
             pltpu.VMEM((2, wide, HEAD_DIM), f32),
-            pltpu.VMEM((2, heads, rows, HEAD_DIM), bf16),
+            pltpu.VMEM((2, 2, heads, rows, HEAD_DIM), bf16),
             pltpu.VMEM((2, n_ctx, heads, wide, 2 * HEAD_DIM), bf16),
             pltpu.VMEM((2, rows, 1), f32),
             pltpu.VMEM((2, rows, 1), f32),

time: 161 us -> 127 us (0.79)
  Pallas kernels: 159 us -> 125 us
    pallas_call x1, Pallas kernels: 159 us -> 125 us  [shards(): pl.pallas_call(functools.partial(fused_kernel, n_groups, n_ctx, n_head),...]
where the time goes in v2:
time: 127 us
  Pallas kernels  125 us (98%)
  local copies, waits for them, and re-layouts  1.87 us (1%)
    pallas_call x1, Pallas kernels, shards(): pl.pallas_call(functools.partial(fused_kernel, n_groups, n_ctx, n_head),...  125 us

profile of v2, /device:TPU:0, one launch (start us, length us, event | category | flops | bytes accessed | tf_op | source)
XLA Modules:
  0.0 126.9 jit_solution(2684990051171655402)
XLA Ops:
  0.0 125.1 %fused.1 = bf16[256,1024]{1,0:T(8,128)(2,1)} custom-call(bf16[2,256,1024]{2,1,0:T(8,128)(2,1)} %hidden.1, s32[1,256]{1,0:T(1,128)} %bitcast.3, s32[1,128]{1,0:T(1,128)} %bitcast.4, s32[1,128]{1,0:T(1,128)} %bitcast.5, bf16[4,4096]{1,0:T(4,128)(2,1)} %embed_in.1, f32[1,128]{1,0:T(1,128)} %constant.2.clone.freq_in, bf16[4096,512]{1,0:T(8,128)(2,1)} %wq.1, ...), custom_call_target="tpu_custom_call" | custom-call | tf_op jit(solution)/shard_map/fused/pallas_call | solution.py:647
  125.1 1.9 %copy.12 = bf16[256,1024]{1,0:T(8,128)(2,1)} copy(bf16[256,1024]{1,0:T(8,128)(2,1)} %fused.1) | data formatting | bytes 1048576

commit v3 on v2

--- a/solution.py
+++ b/solution.py
@@ -82,6 +82,8 @@
     pr_sem,
     ks_sem,
     kr_sem,
+    es_sem,
+    er_sem,
     cs_sem,
     cr_sem,
 ):
@@ -92,6 +94,7 @@
     hw = wq.shape[1]
     heads = hw // HEAD_DIM
     slots = 2 * VAR_DEV
+    wide = rows + slots
     window = rows * n_ctx
     piece = rows // PIECES
     plane = n_groups * n_ctx
@@ -178,8 +181,11 @@
             device_id_type=MESH,
         )
 
-    def send_own(side, strand):
-        for part_id in range(PIECES):
+    rounds = ((0, (0, 1)), (1, (0,)), (1, (1,)))
+
+    def send_own(side, turn):
+        strand, parts = rounds[turn]
+        for part_id in parts:
             hop(side, strand, z, part_id, hidden).start()
 
     @pl.when(z > 0)
@@ -193,10 +199,12 @@
     @pl.when((z > 0) & (z == n_head - 1))
     def _():
         send_own(0, 1)
+        send_own(0, 2)
 
     @pl.when((z < n_head - 1) & (z == 0))
     def _():
         send_own(1, 1)
+        send_own(1, 2)
 
     smalls = [
         pltpu.make_async_copy(source, target, small_sem.at[index])
@@ -317,12 +325,17 @@
         paired = jnp.where(step % 2 == 1, (step + 1) // 2, -((step + 1) // 2))
         return z + jnp.where(step <= 2 * shorter, paired, long_side * (step - shorter))
 
-    def project(strand):
-        acc[...] = jnp.zeros_like(acc)
+    def project(turn):
+        strand, parts = rounds[turn]
+        low, high = parts[0] * piece, (parts[-1] + 1) * piece
+        last = high == rows
+        span = pl.ds(low, high - low)
+        taken = pl.ds(low, (wide if last else high) - low)
+        acc[taken, :] = jnp.zeros((taken.size, 3 * hw), jnp.float32)
 
         def step_body(step, carry):
             shard = shard_of(step)
-            for part_id in range(PIECES):
+            for part_id in parts:
 
                 @pl.when(shard > z)
                 def _():
@@ -340,15 +353,17 @@
                     def _():
                         hop(1, strand, shard, part_id, xbuf).start()
 
-            if strand == 0:
+            if turn < 2:
 
                 @pl.when((shard == n_head - 1) & (z < n_head - 1) & (z > 0))
                 def _():
-                    send_own(0, 1)
+                    send_own(0, turn + 1)
 
                 @pl.when((shard == 0) & (z > 0) & (z < n_head - 1))
                 def _():
-                    send_own(1, 1)
+                    send_own(1, turn + 1)
+
+            if turn == 0:
 
                 @pl.when(step == 1)
                 def _():
@@ -361,17 +376,21 @@
 
                     lax.fori_loop(1, plane, spread, 0)
 
-            block = xbuf[strand, shard]
-            stk[pl.ds(0, rows), :] = block
+            block = xbuf[strand, shard, span, :]
+            stk[span, :] = block
             first = pl.multiple_of(shard * feats, feats)
-            picked = jnp.dot(sel[...], block, preferred_element_type=jnp.float32)
-            stk[pl.ds(rows, slots), :] = (
-                picked + diff[strand, :, pl.ds(first, feats)]
-            ).astype(jnp.bfloat16)
+            cols = pl.ds(first, feats)
+            mutated = diff[strand, :, cols] + jnp.dot(
+                sel[:, span], block, preferred_element_type=jnp.float32
+            )
+            if last:
+                stk[pl.ds(rows, slots), :] = mutated.astype(jnp.bfloat16)
+            else:
+                diff[strand, :, cols] = mutated
             for index in range(3):
-                acc[:, pl.ds(index * hw, hw)] += jnp.dot(
-                    stk[...],
-                    wbuf[index, pl.ds(first, feats), :],
+                acc[taken, pl.ds(index * hw, hw)] += jnp.dot(
+                    stk[taken, :],
+                    wbuf[index, cols, :],
                     preferred_element_type=jnp.float32,
                 )
             return carry
@@ -381,44 +400,70 @@
     passes_on = (me < n_ctx - 1, me > 0)
 
     def pass_kv(strand, shard, head):
+        span = pl.ds(0, wide) if strand == 0 else pl.ds(piece, wide - piece)
         return pltpu.make_async_remote_copy(
-            src_ref=kvbuf.at[strand, shard, head],
-            dst_ref=kvbuf.at[strand, shard, head],
+            src_ref=kvbuf.at[strand, shard, head, span],
+            dst_ref=kvbuf.at[strand, shard, head, span],
             send_sem=ks_sem.at[strand, shard, head],
             recv_sem=kr_sem.at[strand, shard, head],
             device_id={"ctx": me + 1 if strand == 0 else me - 1},
             device_id_type=MESH,
         )
 
-    def rotated(strand, index, head):
-        raw = acc[:, pl.ds(index * hw + head * HEAD_DIM, HEAD_DIM)]
+    def early_kv(shard, step):
+        return pltpu.make_async_remote_copy(
+            src_ref=kvbuf.at[1, shard, :, pl.ds(0, piece)],
+            dst_ref=kvbuf.at[1, shard, :, pl.ds(0, piece)],
+            send_sem=es_sem.at[step - 1],
+            recv_sem=er_sem.at[step - 1],
+            device_id={"ctx": me - step},
+            device_id_type=MESH,
+        )
+
+    def rotated(strand, index, head, span):
+        raw = acc[span, pl.ds(index * hw + head * HEAD_DIM, HEAD_DIM)]
         return (
-            raw * cos[strand] + pltpu.roll(raw, HEAD_DIM // 2, 1) * sin[strand]
+            raw * cos[strand, span, :] + pltpu.roll(raw, HEAD_DIM // 2, 1) * sin[strand, span, :]
         ).astype(jnp.bfloat16)
 
-    def finish(strand):
+    def finish(turn):
+        strand, parts = rounds[turn]
+        low, high = parts[0] * piece, (parts[-1] + 1) * piece
+        last = high == rows
+        taken = pl.ds(low, (wide if last else high) - low)
+
         def send_head(head):
-            @pl.when(passes_on[strand])
-            def _():
-                pass_kv(strand, me, head).start()
+            if last:
+
+                @pl.when(passes_on[strand])
+                def _():
+                    pass_kv(strand, me, head).start()
 
         for head in range(heads):
-            kvbuf[strand, me, head, :, pl.ds(0, HEAD_DIM)] = rotated(strand, 1, head)
-            kvbuf[strand, me, head, :, pl.ds(HEAD_DIM, HEAD_DIM)] = acc[
-                :, pl.ds(2 * hw + head * HEAD_DIM, HEAD_DIM)
+            kvbuf[strand, me, head, taken, pl.ds(0, HEAD_DIM)] = rotated(strand, 1, head, taken)
+            kvbuf[strand, me, head, taken, pl.ds(HEAD_DIM, HEAD_DIM)] = acc[
+                taken, pl.ds(2 * hw + head * HEAD_DIM, HEAD_DIM)
             ].astype(jnp.bfloat16)
             if head:
                 send_head(head - 1)
         for head in range(heads):
-            turned = rotated(strand, 0, head)
-            base = turned[:rows]
-            placed = jnp.dot(sel_t[...], turned[rows:], preferred_element_type=jnp.float32)
-            qbuf[strand, 0, head] = base
-            qbuf[strand, 1, head] = jnp.where(
-                has_row[...] > 0.5, placed, base.astype(jnp.float32)
-            ).astype(jnp.bfloat16)
+            turned = rotated(strand, 0, head, taken)
+            qbuf[strand, 0, head, pl.ds(low, high - low), :] = turned[: high - low]
+            if last:
+                placed = jnp.dot(
+                    sel_t[...], turned[high - low :], preferred_element_type=jnp.float32
+                )
+                qbuf[strand, 1, head] = jnp.where(
+                    has_row[...] > 0.5, placed, qbuf[strand, 0, head].astype(jnp.float32)
+                ).astype(jnp.bfloat16)
             if head == 0:
                 send_head(heads - 1)
+        if not last:
+            for step in range(1, n_ctx):
+
+                @pl.when(me >= step)
+                def _():
+                    early_kv(me, step).start()
 
     def comb_hop(side, shard, head):
         cols = pl.ds(pl.multiple_of(head * HEAD_DIM, HEAD_DIM), HEAD_DIM)
@@ -483,6 +528,12 @@
 
                 @pl.when(shard >= 0 if strand == 0 else shard < n_ctx)
                 def _():
+                    if strand == 1:
+
+                        @pl.when(head == 0)
+                        def _():
+                            early_kv(shard, step).wait_recv()
+
                     pass_kv(strand, shard, head).wait_recv()
 
                     @pl.when(passes_on[strand])
@@ -508,13 +559,15 @@
     at_end = (z == 0) | (z == n_head - 1)
     project(0)
     finish(0)
+    project(1)
+    finish(1)
 
     @pl.when(at_end)
     def _():
         attend(0)
 
-    project(1)
-    finish(1)
+    project(2)
+    finish(2)
 
     @pl.when(jnp.logical_not(at_end))
     def _():
@@ -609,6 +662,11 @@
         return carry
 
     lax.fori_loop(0, n_ctx, drain_ctx, 0)
+    for step in range(1, n_ctx):
+
+        @pl.when(me >= step)
+        def _():
+            early_kv(me, step).wait_send()
 
 
 def anywhere():
@@ -687,6 +745,8 @@
             dma((plane,)),
             dma((2, n_ctx, heads)),
             dma((2, n_ctx, heads)),
+            dma((max(n_ctx - 1, 1),)),
+            dma((max(n_ctx - 1, 1),)),
             dma((2, n_head, heads)),
             dma((n_head, heads)),
         ],

time: 127 us -> 123 us (0.969)
  Pallas kernels: 125 us -> 121 us
    pallas_call x1, Pallas kernels: 125 us -> 121 us  [shards(): pl.pallas_call(functools.partial(fused_kernel, n_groups, n_ctx, n_head),...]
where the time goes in v3:
time: 123 us
  Pallas kernels  121 us (98%)
  local copies, waits for them, and re-layouts  1.87 us (2%)
    pallas_call x1, Pallas kernels, shards(): pl.pallas_call(functools.partial(fused_kernel, n_groups, n_ctx, n_head),...  121 us

profile of v3, /device:TPU:0, one launch (start us, length us, event | category | flops | bytes accessed | tf_op | source)
XLA Modules:
  0.0 123.2 jit_solution(19329442518077547)
XLA Ops:
  0.0 121.3 %fused.1 = bf16[256,1024]{1,0:T(8,128)(2,1)} custom-call(bf16[2,256,1024]{2,1,0:T(8,128)(2,1)} %hidden.1, s32[1,256]{1,0:T(1,128)} %bitcast.3, s32[1,128]{1,0:T(1,128)} %bitcast.4, s32[1,128]{1,0:T(1,128)} %bitcast.5, bf16[4,4096]{1,0:T(4,128)(2,1)} %embed_in.1, f32[1,128]{1,0:T(1,128)} %constant.2.clone.freq_in, bf16[4096,512]{1,0:T(8,128)(2,1)} %wq.1, ...), custom_call_target="tpu_custom_call" | custom-call | tf_op jit(solution)/shard_map/fused/pallas_call | solution.py:705
  121.3 1.9 %copy.12 = bf16[256,1024]{1,0:T(8,128)(2,1)} copy(bf16[256,1024]{1,0:T(8,128)(2,1)} %fused.1) | data formatting | bytes 1048576

commit v4 on v3

--- a/solution.py
+++ b/solution.py
@@ -491,34 +491,41 @@
         def update(shard, head, first):
             k_times = (clock(strand, row_row + (shard * rows).astype(jnp.float32)), kt[strand, shard])
             spans = (rows, rows + slots)
-            for kind in range(2):
-                span = pl.ds(0, spans[kind])
-                raw = lax.dot_general(
+            raws = [
+                lax.dot_general(
                     qbuf[strand, kind, head],
-                    kvbuf[strand, shard, head, span, pl.ds(0, HEAD_DIM)],
+                    kvbuf[strand, shard, head, pl.ds(0, spans[kind]), pl.ds(0, HEAD_DIM)],
                     (((1,), (1,)), ((), ())),
                     preferred_element_type=jnp.float32,
                 )
-                if first or kind == 1:
+                for kind in range(2)
+            ]
+            weighted = []
+            for kind in range(2):
+                raw = raws[kind]
+                if first:
                     raw = jnp.where(k_times[kind] <= q_time, raw, NEG_FILL)
+                elif kind:
+                    raw = jnp.where(k_times[kind] < 0.5 * FAR, raw, NEG_FILL)
                 top = jnp.max(raw, axis=1, keepdims=True)
+                fade = None
                 if not first:
                     before = m_buf[kind]
                     top = jnp.maximum(before, top)
                     fade = jnp.exp2((before - top) * log_scale)
                 weights = jnp.exp2((raw - top) * log_scale)
                 total = jnp.sum(weights, axis=1, keepdims=True)
+                m_buf[kind] = top
+                l_buf[kind] = total if first else total + fade * l_buf[kind]
+                weighted.append((weights.astype(jnp.bfloat16), fade))
+            for kind in range(2):
+                weights, fade = weighted[kind]
                 vec = jnp.dot(
-                    weights.astype(jnp.bfloat16),
-                    kvbuf[strand, shard, head, span, pl.ds(HEAD_DIM, HEAD_DIM)],
+                    weights,
+                    kvbuf[strand, shard, head, pl.ds(0, spans[kind]), pl.ds(HEAD_DIM, HEAD_DIM)],
                     preferred_element_type=jnp.float32,
                 )
-                if not first:
-                    total = total + fade * l_buf[kind]
-                    vec = vec + fade * a_buf[kind]
-                m_buf[kind] = top
-                l_buf[kind] = total
-                a_buf[kind] = vec
+                a_buf[kind] = vec if first else vec + fade * a_buf[kind]
 
         def one_head(head, carry):
             update(me, head, True)

time: 123 us -> 122 us (level)
    pallas_call x1, Pallas kernels: 121 us -> 120 us  [shards(): pl.pallas_call(functools.partial(fused_kernel, n_groups, n_ctx, n_head),...]
where the time goes in v4:
time: 122 us
  Pallas kernels  120 us (98%)
  local copies, waits for them, and re-layouts  1.87 us (2%)
    pallas_call x1, Pallas kernels, shards(): pl.pallas_call(functools.partial(fused_kernel, n_groups, n_ctx, n_head),...  120 us

profile of v4, /device:TPU:0, one launch (start us, length us, event | category | flops | bytes accessed | tf_op | source)
XLA Modules:
  0.0 121.7 jit_solution(8545595970484984527)
XLA Ops:
  0.0 119.9 %fused.1 = bf16[256,1024]{1,0:T(8,128)(2,1)} custom-call(bf16[2,256,1024]{2,1,0:T(8,128)(2,1)} %hidden.1, s32[1,256]{1,0:T(1,128)} %bitcast.3, s32[1,128]{1,0:T(1,128)} %bitcast.4, s32[1,128]{1,0:T(1,128)} %bitcast.5, bf16[4,4096]{1,0:T(4,128)(2,1)} %embed_in.1, f32[1,128]{1,0:T(1,128)} %constant.2.clone.freq_in, bf16[4096,512]{1,0:T(8,128)(2,1)} %wq.1, ...), custom_call_target="tpu_custom_call" | custom-call | tf_op jit(solution)/shard_map/fused/pallas_call | solution.py:712
  119.9 1.9 %copy.12 = bf16[256,1024]{1,0:T(8,128)(2,1)} copy(bf16[256,1024]{1,0:T(8,128)(2,1)} %fused.1) | data formatting | bytes 1048576
